TPU v7x, 32 devices: a whole 2x2x4 slice. The times are simulated.
32 devices in a mesh: ctx: 4 (over y, core), head: 2 (over x), dp: 4 (over z).
Axes of the slice: x: 2, y: 2, z: 4, core: 2. Of those that a mesh axis runs over, the one named last changes fastest.
Arguments:
- queries: bfloat16 [1024, 6144], P(('dp', 'ctx', 'head')), parts along dimension 0, may hold values from -18 to 18
- keys: bfloat16 [1024, 1024], P(('dp', 'ctx', 'head')), parts along dimension 0, may hold values from -9 to 9
- values: bfloat16 [1024, 1024], P(('dp', 'ctx', 'head')), parts along dimension 0, may hold values from -6 to 6
- level_gain: float32 [64, 6144], P(None, 'head'), may hold values from 0.5 to 4
- levels: int32 [16], P('dp'), parts along dimension 0, may hold values from 0 to 63
- visible: int32 [16, 4], P('dp'), parts along dimension 0, may hold values from 0 to 1, as said below
- counts: int32 [16], P('dp'), parts along dimension 0, may hold values from 32 to 64, as said below
Outputs:
- mixed: bfloat16 [1024, 6144], P(('dp', 'ctx', 'head')), parts along dimension 0
- finished: bfloat16 [256, 6144], P(('dp', 'ctx'), 'head'), parts along dimension 0
There are 4 independent parts, one for each index of `dp`. A program takes and returns all parts, laid end to end along the dimension named above; an argument that names none is the same for every part. Nothing has to cross between parts.
Inputs may be any that keep to these rules, and one draw needn't show every extreme that they name: visible[c][c] is 1, visible[c][d] is 0 for d > c, and entries below the diagonal are 0 or 1. `counts`: every clip has at least half of its slots live, and in every draw some clip has all 64 live.
All inputs are finite; a program needn't handle non-finite values.
Results may differ from a plain program's by a relative error of at most 0.0045.
Values may be sent and summed in bfloat16 or wider, within the bound.
No kernel may reach another device: no remote copies, remote signals or barrier semaphores. Data moves between devices by JAX's collectives and lax.ppermute only.
A program may use at most 64 MiB of HBM per device.

v0:
```python
import math
import jax
import jax.numpy as jnp
from jax import lax
from jax.sharding import PartitionSpec as P

QUERY_HEADS = 48
KEY_VALUE_HEADS = 8
HEAD_SIZE = 128
LEVELS = 64
CLIPS = 4


def from_behind(block, axis, distance):
    devices = range(lax.axis_size(axis))
    route = [(i - distance, i) for i in devices if i - distance in devices]
    return lax.ppermute(block, axis, route)


def body(queries, keys, values, level_gain, levels, visible, counts):
    head_count = lax.axis_size("head")
    ctx_count = lax.axis_size("ctx")
    ctx_index = lax.axis_index("ctx")
    tok_rows = queries.shape[0]
    rows_ctx = tok_rows * head_count
    clip_tok = rows_ctx * ctx_count // CLIPS
    heads_per_group = QUERY_HEADS // KEY_VALUE_HEADS
    scale = 1.0 / math.sqrt(HEAD_SIZE)
    clip_range = jnp.arange(CLIPS, dtype=jnp.int32)
    source_count = ctx_count // CLIPS
    query_local, key_local, value_local = (
        lax.all_to_all(queries, "head", split_axis=1, concat_axis=0, tiled=True),
        lax.all_to_all(keys, "head", split_axis=1, concat_axis=0, tiled=True),
        lax.all_to_all(values, "head", split_axis=1, concat_axis=0, tiled=True),
    )
    query_width = query_local.shape[1]
    query_ids = ctx_index * rows_ctx + jnp.arange(rows_ctx, dtype=jnp.int32)
    row_groups = [(0, rows_ctx)]
    query_grouped = query_local.reshape(rows_ctx, -1, heads_per_group, HEAD_SIZE)
    local_kv_heads = query_grouped.shape[1]
    query_onehot = (query_ids // clip_tok)[:, None] == clip_range[None, :]
    query_count = jnp.sum(jnp.where(query_onehot, counts[None, :], 0), axis=1)
    query_live = query_ids % clip_tok < query_count
    query_sees = jnp.sum(jnp.where(query_onehot[:, :, None], visible[None, :, :], 0), axis=1) == 1
    query_level = jnp.sum(jnp.where(query_onehot, levels[None, :], 0), axis=1)

    def key_block(carry_state, key_block_rows, value_block_rows, first_row):
        block_rows = key_block_rows.shape[0]
        key_ids = first_row + jnp.arange(block_rows, dtype=jnp.int32)
        key_onehot = (key_ids // clip_tok)[:, None] == clip_range[None, :]
        key_count = jnp.sum(jnp.where(key_onehot, counts[None, :], 0), axis=1)
        key_live = key_ids % clip_tok < key_count
        block_clips = jnp.any(key_onehot & key_live[:, None], axis=0)
        key_head_rows = key_block_rows.reshape(block_rows, -1, HEAD_SIZE)
        value_head_rows = value_block_rows.reshape(block_rows, -1, HEAD_SIZE)
        group_start, group_rows = row_groups[0]
        group_end = group_start + group_rows
        part_state = tuple((member for member in carry_state))
        group_sees = query_sees
        needed = jnp.any(jnp.any(group_sees, axis=0) & block_clips)

        def update(state, group_sees=group_sees, group_start=group_start, group_end=group_end):
            running_max, denominator, weighted = state
            allowed = (
                jnp.any(group_sees[:, None, :] & key_onehot[None, :, :], axis=-1)
                & key_live[None, :]
            )
            scores = (
                jnp.einsum(
                    "rkgd,nkd->rkgn",
                    query_grouped,
                    key_head_rows,
                    preferred_element_type=jnp.float32,
                )
                * scale
            )
            key_mask = allowed[:, None, None, :]
            scores = jnp.where(key_mask, scores, -1e30)
            new_max = jnp.maximum(running_max, jnp.max(scores, axis=-1))
            weights = jnp.where(key_mask, jnp.exp(scores - new_max[..., None]), 0.0)
            shrink = jnp.exp(running_max - new_max)
            denominator = denominator * shrink + jnp.sum(weights, axis=-1)
            weighted = weighted * shrink[..., None] + jnp.einsum(
                "rkgn,nkd->rkgd",
                weights.astype(jnp.bfloat16),
                value_head_rows,
                preferred_element_type=jnp.float32,
            )
            return (new_max, denominator, weighted)

        def keep(state):
            return state

        group_states = [lax.cond(needed, update, keep, part_state)]
        if len(group_states) == 1:
            return group_states[0]
        return tuple(
            (
                jnp.concatenate([state[member] for state in group_states], axis=0)
                for member in range(3)
            )
        )

    initial = (
        jnp.full((rows_ctx, local_kv_heads, heads_per_group), -1e30, jnp.float32),
        jnp.zeros((rows_ctx, local_kv_heads, heads_per_group), jnp.float32),
        jnp.zeros((rows_ctx, local_kv_heads, heads_per_group, HEAD_SIZE), jnp.float32),
    )
    key_piece = lax.all_gather(key_local, "ctx", axis=0, tiled=True)
    value_piece = lax.all_gather(value_local, "ctx", axis=0, tiled=True)
    piece_rows = key_piece.shape[0]
    block_rows = math.gcd(piece_rows, 512)

    def advance(block_index, inner_state):
        key_slice = lax.dynamic_slice_in_dim(key_piece, block_index * block_rows, block_rows, 0)
        value_slice = lax.dynamic_slice_in_dim(value_piece, block_index * block_rows, block_rows, 0)
        return key_block(inner_state, key_slice, value_slice, block_index * block_rows)

    final_state = lax.fori_loop(0, piece_rows // block_rows, advance, initial)
    attended = (final_state[2] / final_state[1][..., None]).reshape(rows_ctx, query_width)
    level_onehot = (query_level[:, None] == jnp.arange(LEVELS, dtype=jnp.int32)[None, :]).astype(
        jnp.float32
    )
    gate_rows = jnp.dot(
        level_onehot,
        level_gain,
        precision=lax.Precision.HIGHEST,
        preferred_element_type=jnp.float32,
    )
    gated = jnp.where(query_live[:, None], attended * gate_rows, 0.0).astype(jnp.bfloat16)
    mixed = lax.all_to_all(gated, "head", split_axis=0, concat_axis=1, tiled=True)
    relay_rows = rows_ctx // CLIPS
    held = jnp.where(ctx_index < source_count, gated, jnp.zeros_like(gated)).reshape(
        CLIPS, relay_rows, query_width
    )
    empty_block = jnp.zeros_like(held)
    sources = jnp.arange(source_count, dtype=jnp.int32)
    hop_bits = (source_count - 1).bit_length()
    for bit_number in reversed(range(hop_bits)):
        higher = sources >> bit_number + 1 << bit_number + 1
        places = sources + 3 * higher
        holds_bit = jnp.any((places == ctx_index) & (sources >> bit_number & 1 == 1))
        moving = jnp.where(holds_bit, held, empty_block)
        staying = jnp.where(holds_bit, empty_block, held)
        arriving = from_behind(moving, "ctx", 3 * (1 << bit_number))
        held = staying + arriving
    group_position = ctx_index % CLIPS
    finished = held[0]
    for lane_number in range(1, CLIPS):
        arriving_tile = from_behind(held[lane_number], "ctx", lane_number)
        finished = jnp.where(group_position == lane_number, arriving_tile, finished)
    return (mixed, finished)


def solution(mesh):
    placed = (
        P(("dp", "ctx", "head"), None),
        P(("dp", "ctx", "head"), None),
        P(("dp", "ctx", "head"), None),
        P(None, "head"),
        P("dp"),
        P("dp", None),
        P("dp"),
    )
    return jax.shard_map(
        body,
        mesh=mesh,
        in_specs=placed,
        out_specs=(P(("dp", "ctx", "head"), None), P(("dp", "ctx"), "head")),
        check_vma=False,
    )
```

profile of v0, /device:TPU:0, one launch (start us, length us, event | category | flops | bytes accessed | tf_op | source)
XLA Modules:
  0.0 61.5 jit_solution(9454937511669953927)
XLA Ops:
  0.6 1.5 %copy.71 = bf16[4,2,8,512]{3,2,0,1:T(8,128)(2,1)} copy(bf16[4,2,8,512]{3,2,1,0:T(8,128)(2,1)} %bitcast.40) | data formatting | bytes 131072 | tf_op jit(solution)/shard_map/all_to_all | solution.py:33
  2.2 4.2 %all-to-all-start = ((bf16[32,2,512]{2,0,1:T(8,128)(2,1)}), bf16[32,2,512]{2,0,1:T(8,128)(2,1)S(1)}, u32[]{:S(2)}, u32[]{:S(2)}) async-start(bf16[32,2,512]{2,0,1:T(8,128)(2,1)} %bitcast.31), calls=%async_computation | async-start | bytes 131072 | tf_op jit(solution)/shard_map/all_to_all | solution.py:33
  6.5 0.8 %select_reduce_fusion = s32[64,4]{0,1:T(4,128)S(1)} fusion(s32[4,4]{1,0:T(4,128)} %param.14, pred[64,4]{0,1:T(4,128)(4,1)S(1)} %iota_compare_fusion.3), kind=kLoop, calls=%fused_computation.33 | loop fusion | flops 1792 | bytes 1344 | tf_op jit(solution)/shard_map/reduce_sum | solution.py:44
  7.3 0.7 %select_reduce_fusion.1 = s32[256]{0:T(256)S(1)} fusion(s32[4]{0:T(128)} %param.15, s32[256]{0:T(256)S(1)} %and_select_fusion.2), kind=kLoop, calls=%fused_computation.34 | loop fusion | flops 2816 | bytes 2064 | tf_op jit(solution)/shard_map/while/body/eval_jaxpr/reduce_sum | solution.py:51
  8.1 0.1 iota_compare_fusion.2
  8.2 0.8 %select_reduce_fusion.2 = (s32[64]{0:T(128)S(1)}, s32[64]{0:T(128)S(1)}) fusion(s32[4]{0:T(128)} %param.13, s32[64]{0:T(128)S(1)} %and_select_fusion.3, s32[4]{0:T(128)} %param.15), kind=kLoop, calls=%fused_computation.37 | loop fusion | flops 1152 | bytes 800 | tf_op jit(solution)/shard_map/reduce_sum | solution.py:45
  9.0 0.6 %and_reduce_fusion.2 = pred[]{:T(512)} fusion(pred[4]{0:T(512)(128)(4,1)S(1)} %get-tuple-element.148, pred[4]{0:T(512)(128)(4,1)S(1)} %get-tuple-element.158), kind=kLoop, calls=%fused_computation.43 | loop fusion | flops 7 | bytes 9 | tf_op jit(solution)/shard_map/while/body/eval_jaxpr/reduce_or | solution.py:60
  9.6 1.5 %copy.70 = bf16[4,2,8,512]{3,2,0,1:T(8,128)(2,1)} copy(bf16[4,2,8,512]{3,2,1,0:T(8,128)(2,1)} %bitcast.41) | data formatting | bytes 131072 | tf_op jit(solution)/shard_map/all_to_all | solution.py:34
  11.1 3.3 %all-to-all-start.2 = ((bf16[32,2,512]{2,0,1:T(8,128)(2,1)}), bf16[32,2,512]{2,0,1:T(8,128)(2,1)S(1)}, u32[]{:S(2)}, u32[]{:S(2)}) async-start(bf16[32,2,512]{2,0,1:T(8,128)(2,1)} %bitcast.30), calls=%async_computation.2 | async-start | bytes 131072 | tf_op jit(solution)/shard_map/all_to_all | solution.py:34
  15.1 1.8 %copy.69 = bf16[4,2,8,3072]{3,2,0,1:T(8,128)(2,1)} copy(bf16[4,2,8,3072]{3,2,1,0:T(8,128)(2,1)} %bitcast.35) | data formatting | bytes 786432 | tf_op jit(solution)/shard_map/all_to_all | solution.py:32
  16.9 1.6 %all-to-all-done.2 = bf16[32,2,512]{2,0,1:T(8,128)(2,1)S(1)} async-done(((bf16[32,2,512]{2,0,1:T(8,128)(2,1)}), bf16[32,2,512]{2,0,1:T(8,128)(2,1)S(1)}, u32[]{:S(2)}, u32[]{:S(2)}) %all-to-all-start.2) | async-done | bytes 65568 | tf_op jit(solution)/shard_map/all_to_all | solution.py:34
  18.5 3.5 %all-to-all-start.1 = ((bf16[32,2,3072]{2,0,1:T(8,128)(2,1)}), bf16[32,2,3072]{2,0,1:T(8,128)(2,1)S(1)}, u32[]{:S(2)}, u32[]{:S(2)}) async-start(bf16[32,2,3072]{2,0,1:T(8,128)(2,1)} %bitcast.29), calls=%async_computation.1 | async-start | bytes 786432 | tf_op jit(solution)/shard_map/all_to_all | solution.py:32
  22.0 6.3 %all_gather.6 = bf16[256,512]{1,0:T(8,128)(2,1)S(1)} all-gather(bf16[64,512]{1,0:T(8,128)(2,1)S(1)} %bitcast.37), channel_id=1, replica_groups=mesh['ctx'=4,'head'=2,'dp'=4] {'ctx'}, dimensions={0}, use_global_device_ids=true | all-gather | bytes 327680 | tf_op jit(solution)/shard_map/all_gather | solution.py:109
  28.3 5.8 %all_gather.7 = bf16[256,512]{1,0:T(8,128)(2,1)S(1)} all-gather(bf16[64,512]{1,0:T(8,128)(2,1)S(1)} %bitcast.38), channel_id=1, replica_groups=mesh['ctx'=4,'head'=2,'dp'=4] {'ctx'}, dimensions={0}, use_global_device_ids=true | all-gather | bytes 327680 | tf_op jit(solution)/shard_map/all_gather | solution.py:110
  34.2 6.7 %conditional.1 = ((f32[64,4,6]{0,2,1:T(8,128)S(1)}, f32[64,4,6,128]{3,0,2,1:T(8,128)S(1)})) conditional(s32[]{:T(128)} %convert_element_type.13, (f32[64,4,6]{0,2,1:T(8,128)S(1)}, f32[64,4,6,128]{3,0,2,1:T(8,128)S(1)}) %tuple.31, (pred[64,4]{0,1:T(4,128)(4,1)S(1)}, pred[256,4]{0,1:T(4,128)(4,1)S(1)}, s32[256]{0:T(256)S(1)}, s32[256]{0:T(256)S(1)}, ...), branch_computations={%region_6.7_spmd, %region_7.11_spmd} | conditional | flops 205395968 | bytes 9220888 | solution.py:94
  34.2 1.3 %reshape.148 = bf16[64,4,6,128]{3,2,1,0:T(8,128)(2,1)} reshape(bf16[2,32,3072]{2,1,0:T(8,128)(2,1)S(1)} %get-tuple-element.127) | data formatting | bytes 786432 | tf_op jit(solution)/shard_map/reshape | solution.py:39
  35.4 0.8 %reshape.147 = bf16[256,4,128]{2,1,0:T(4,128)(2,1)} reshape(bf16[256,512]{1,0:T(8,128)(2,1)S(1)} %get-tuple-element.126) | data formatting | bytes 524288 | tf_op jit(solution)/shard_map/while/body/eval_jaxpr/reshape | solution.py:54
  36.4 1.6 %fusion.21 = (f32[64,4,6]{0,2,1:T(8,128)S(1)}, f32[64,4,6,256]{3,0,2,1:T(8,128)S(1)}) fusion(bf16[64,4,6,128]{3,2,1,0:T(8,128)(2,1)} %reshape.148, bf16[256,4,128,1]{2,1,0,3:T(4,128)(2,1)} %bitcast.39, pred[64,256]{1,0:T(8,128)(4,1)S(1)} %broadcast_and_fusion), kind=kOutput, calls=%fused_computation.57 | convolution fusion | flops 101841408 | bytes 2250752 | tf_op jit(solution)/shard_map/while/body/eval_jaxpr/cond/branch_1_fun/rkgd,nkd->rkgn/dot_general | solution.py:69
  38.0 0.5 fusion.2
  38.6 0.8 %reshape.149 = bf16[256,4,128]{2,1,0:T(4,128)(2,1)} reshape(bf16[256,512]{1,0:T(8,128)(2,1)S(1)} %get-tuple-element.129) | data formatting | bytes 524288 | tf_op jit(solution)/shard_map/while/body/eval_jaxpr/reshape | solution.py:55
  39.3 1.6 %fusion = f32[64,4,6,128]{3,0,2,1:T(8,128)S(1)} fusion(f32[64,4,6,256]{3,0,2,1:T(8,128)S(1)} %get-tuple-element.153, f32[64,4,6,128]{3,0,2,1:T(8,128)S(1)} %get-tuple-element.128, f32[64,4,6]{0,2,1:T(8,128)S(1)} %broadcast_maximum_fusion, pred[64,256]{1,0:T(8,128)(4,1)S(1)} %broadcast_and_fusion, f32[64,4,6]{0,2,1:T(8,128)S(1)} %get-tuple-element.150, ...), kind=kOutput, calls=%fused_computation.3 | convolution fusion | flops 102236160 | bytes 3436544 | tf_op jit(solution)/shard_map/while/body/eval_jaxpr/cond/branch_1_fun/rkgn,nkd->rkgd/dot_general | solution.py:83
  40.9 0.3 broadcast_divide_fusion
  41.2 0.5 copy.44
  41.7 0.2 reshape.151
  41.9 1.3 %broadcast_select_fusion = (bf16[64,3072]{1,0:T(8,128)(2,1)S(1)}, bf16[64,3072]{1,0:T(8,128)(2,1)}) fusion(pred[]{:T(512)S(6)} %lt.53, f32[64,3072]{1,0:T(8,128)S(1)} %reshape.151, f32[64,3072]{1,0:T(8,128)S(1)} %copy-done, s32[64]{0:T(128)S(1)} %get-tuple-element.146, pred[64]{0:T(512)(128)(4,1)S(1)} %fusion.19), kind=kOutput, calls=%fused_computation.25 | convolution fusion | flops 151785472 | bytes 2359617 | tf_op jit(solution)/shard_map/dot_general | solution.py:124
  43.2 3.4 %collective-permute-start = (bf16[16,3072]{1,0:T(8,128)(2,1)S(1)}, bf16[16,3072]{1,0:T(8,128)(2,1)S(1)}, u32[]{:S(2)}, u32[]{:S(2)}) collective-permute-start(bf16[16,3072]{1,0:T(8,128)(2,1)S(1)} %get-tuple-element.156), channel_id=1, source_target_pairs={{0,24},{1,25},{2,26},{3,27},{4,28},{5,29},{6,30},{7,31}} | collective-permute-start | bytes 294920 | tf_op jit(solution)/shard_map/ppermute | solution.py:17
  46.6 1.3 %collective-permute-start.1 = (bf16[16,3072]{1,0:T(8,128)(2,1)S(1)}, bf16[16,3072]{1,0:T(8,128)(2,1)S(1)}, u32[]{:S(2)}, u32[]{:S(2)}) collective-permute-start(bf16[16,3072]{1,0:T(8,128)(2,1)S(1)} %get-tuple-element.155), channel_id=1, source_target_pairs={{0,16},{8,24},{1,17},{9,25},{2,18},{10,26},{3,19},{11,27},{4,20},{... | collective-permute-start | bytes 294920 | tf_op jit(solution)/shard_map/ppermute | solution.py:17
  47.9 2.0 %collective-permute-start.2 = (bf16[16,3072]{1,0:T(8,128)(2,1)S(1)}, bf16[16,3072]{1,0:T(8,128)(2,1)S(1)}, u32[]{:S(2)}, u32[]{:S(2)}) collective-permute-start(bf16[16,3072]{1,0:T(8,128)(2,1)S(1)} %get-tuple-element.154), channel_id=1, source_target_pairs={{0,8},{8,16},{16,24},{1,9},{9,17},{17,25},{2,10},{10,18},{18,26},{... | collective-permute-start | bytes 294920 | tf_op jit(solution)/shard_map/ppermute | solution.py:17
  50.0 3.5 %all-to-all-start.3 = ((bf16[2,32,3072]{2,1,0:T(8,128)(2,1)}), bf16[2,32,3072]{2,1,0:T(8,128)(2,1)S(1)}, u32[]{:S(2)}, u32[]{:S(2)}) async-start(bf16[2,32,3072]{2,1,0:T(8,128)(2,1)} %bitcast.9), calls=%async_computation.3 | async-start | bytes 786432 | tf_op jit(solution)/shard_map/all_to_all | solution.py:131
  53.5 0.7 %fusion.15 = bf16[16,3072]{1,0:T(8,128)(2,1)} fusion(bf16[16,3072]{1,0:T(8,128)(2,1)S(1)} %collective-permute-done, bf16[16,3072]{1,0:T(8,128)(2,1)S(1)} %collective-permute-done.1, bf16[16,3072]{1,0:T(8,128)(2,1)S(1)} %collective-permute-done.2, bf16[64,3072]{1,0:T(8,128)(2,1)S(1)} %get-tuple-element.159, pred[]{:T(512)S(6)} %eq.97, pred[]{:T(512)S(6)} %eq.96, ...), kind=kLoop, calls=%fused_computation.28 | loop fusion | flops 147456 | bytes 491523 | tf_op jit(solution)/shard_map/jit(_where)/select_n | solution.py:151
  54.1 6.6 %all-to-all-done.3 = bf16[2,32,3072]{2,1,0:T(8,128)(2,1)S(1)} async-done(((bf16[2,32,3072]{2,1,0:T(8,128)(2,1)}), bf16[2,32,3072]{2,1,0:T(8,128)(2,1)S(1)}, u32[]{:S(2)}, u32[]{:S(2)}) %all-to-all-start.3) | async-done | bytes 393248 | tf_op jit(solution)/shard_map/all_to_all | solution.py:131
  60.7 0.8 %copy.55 = bf16[2,4,8,3072]{3,2,0,1:T(8,128)(2,1)} copy(bf16[2,4,8,3072]{3,2,1,0:T(8,128)(2,1)S(1)} %bitcast.33) | data formatting | bytes 786432 | tf_op jit(solution)/shard_map/all_to_all | solution.py:131
  (23 shorter events, 0.4 us)
Async XLA Ops:
  0.6 41.2 %copy-start = (f32[64,3072]{1,0:T(8,128)S(1)}, f32[64,3072]{1,0:T(8,128)}, u32[]{:S(2)}) copy-start(f32[64,3072]{1,0:T(8,128)} %param.12) | copy-start | bytes 2359300
  2.2 8.9 %all-to-all-start = ((bf16[32,2,512]{2,0,1:T(8,128)(2,1)}), bf16[32,2,512]{2,0,1:T(8,128)(2,1)S(1)}, u32[]{:S(2)}, u32[]{:S(2)}) async-start(bf16[32,2,512]{2,0,1:T(8,128)(2,1)} %bitcast.31), calls=%async_computation | async-start | bytes 131072 | tf_op jit(solution)/shard_map/all_to_all | solution.py:33
  11.1 7.4 %all-to-all-start.2 = ((bf16[32,2,512]{2,0,1:T(8,128)(2,1)}), bf16[32,2,512]{2,0,1:T(8,128)(2,1)S(1)}, u32[]{:S(2)}, u32[]{:S(2)}) async-start(bf16[32,2,512]{2,0,1:T(8,128)(2,1)} %bitcast.30), calls=%async_computation.2 | async-start | bytes 131072 | tf_op jit(solution)/shard_map/all_to_all | solution.py:34
  18.5 15.6 %all-to-all-start.1 = ((bf16[32,2,3072]{2,0,1:T(8,128)(2,1)}), bf16[32,2,3072]{2,0,1:T(8,128)(2,1)S(1)}, u32[]{:S(2)}, u32[]{:S(2)}) async-start(bf16[32,2,3072]{2,0,1:T(8,128)(2,1)} %bitcast.29), calls=%async_computation.1 | async-start | bytes 786432 | tf_op jit(solution)/shard_map/all_to_all | solution.py:32
  43.2 10.2 %collective-permute-start = (bf16[16,3072]{1,0:T(8,128)(2,1)S(1)}, bf16[16,3072]{1,0:T(8,128)(2,1)S(1)}, u32[]{:S(2)}, u32[]{:S(2)}) collective-permute-start(bf16[16,3072]{1,0:T(8,128)(2,1)S(1)} %get-tuple-element.156), channel_id=1, source_target_pairs={{0,24},{1,25},{2,26},{3,27},{4,28},{5,29},{6,30},{7,31}} | collective-permute-start | bytes 294920 | tf_op jit(solution)/shard_map/ppermute | solution.py:17
  46.6 6.8 %collective-permute-start.1 = (bf16[16,3072]{1,0:T(8,128)(2,1)S(1)}, bf16[16,3072]{1,0:T(8,128)(2,1)S(1)}, u32[]{:S(2)}, u32[]{:S(2)}) collective-permute-start(bf16[16,3072]{1,0:T(8,128)(2,1)S(1)} %get-tuple-element.155), channel_id=1, source_target_pairs={{0,16},{8,24},{1,17},{9,25},{2,18},{10,26},{3,19},{11,27},{4,20},{... | collective-permute-start | bytes 294920 | tf_op jit(solution)/shard_map/ppermute | solution.py:17
  47.9 5.6 %collective-permute-start.2 = (bf16[16,3072]{1,0:T(8,128)(2,1)S(1)}, bf16[16,3072]{1,0:T(8,128)(2,1)S(1)}, u32[]{:S(2)}, u32[]{:S(2)}) collective-permute-start(bf16[16,3072]{1,0:T(8,128)(2,1)S(1)} %get-tuple-element.154), channel_id=1, source_target_pairs={{0,8},{8,16},{16,24},{1,9},{9,17},{17,25},{2,10},{10,18},{18,26},{... | collective-permute-start | bytes 294920 | tf_op jit(solution)/shard_map/ppermute | solution.py:17
  50.0 10.7 %all-to-all-start.3 = ((bf16[2,32,3072]{2,1,0:T(8,128)(2,1)}), bf16[2,32,3072]{2,1,0:T(8,128)(2,1)S(1)}, u32[]{:S(2)}, u32[]{:S(2)}) async-start(bf16[2,32,3072]{2,1,0:T(8,128)(2,1)} %bitcast.9), calls=%async_computation.3 | async-start | bytes 786432 | tf_op jit(solution)/shard_map/all_to_all | solution.py:131
where the time goes:
time: 62.2 us; the launch traced here: 61.5 us
  starting transfers between devices  21.2 us (34%)
  blocking collectives  12.1 us (19%)
  local copies, waits for them, and re-layouts  9.12 us (15%)
  waiting for transfers between devices  8.19 us (13%)
  other arithmetic  4.82 us (8%)
  matrix products  4.5 us (7%)
  between operations  1.43 us (2%)
    ppermute x3, starting transfers between devices, from_behind(): return lax.ppermute(block, axis, route)  6.7 us
    all_to_all x1, waiting for transfers between devices, body(): lax.all_to_all(gated, 'head', split_axis=0, concat_axis=1, tiled=True)  6.56 us
    all_gather x1, blocking collectives, body(): key_piece = lax.all_gather(key_local, 'ctx', axis=0, tiled=True)  6.31 us
    all_gather x1, blocking collectives, body(): value_piece = lax.all_gather(value_local, 'ctx', axis=0, tiled=True)  5.84 us
    all_to_all x1, starting transfers between devices, body(): lax.all_to_all(keys, 'head', split_axis=1, concat_axis=0, tiled=True)  4.23 us
    all_to_all x1, starting transfers between devices, body(): lax.all_to_all(gated, 'head', split_axis=0, concat_axis=1, tiled=True)  3.48 us
    all_to_all x1, starting transfers between devices, body(): lax.all_to_all(queries, 'head', split_axis=1, concat_axis=0, tiled=True)  3.47 us
    all_to_all x1, starting transfers between devices, body(): lax.all_to_all(values, 'head', split_axis=1, concat_axis=0, tiled=True)  3.32 us
  transfers between devices with their start and end apart: 7, of which 2 were waited for; matrix products, arithmetic and copies ran while one was open for 12% of the time, Pallas kernels for 0%

commit v1 on v0

--- a/solution.py
+++ b/solution.py
@@ -9,6 +9,26 @@
 HEAD_SIZE = 128
 LEVELS = 64
 CLIPS = 4
+
+
+def map_unit(here_x, a_name, join_dim):
+    tile_out = jax.lax.axis_size(a_name)
+    high = jax.lax.axis_index(a_name)
+    fresh, ready, value_now = (tile_out, high, here_x.shape[join_dim])
+    piece_now, arr_out = (here_x, 1)
+    while arr_out < fresh:
+        piece_now = jnp.concatenate(
+            [
+                piece_now,
+                jax.lax.ppermute(
+                    piece_now, a_name, [(ii, (ii - arr_out) % fresh) for ii in range(fresh)]
+                ),
+            ],
+            join_dim,
+        )
+        arr_out = 2 * arr_out
+    back = jnp.roll(piece_now, shift=ready * value_now, axis=join_dim)
+    return back
 
 
 def from_behind(block, axis, distance):
@@ -107,7 +127,7 @@
         jnp.zeros((rows_ctx, local_kv_heads, heads_per_group, HEAD_SIZE), jnp.float32),
     )
     key_piece = lax.all_gather(key_local, "ctx", axis=0, tiled=True)
-    value_piece = lax.all_gather(value_local, "ctx", axis=0, tiled=True)
+    value_piece = map_unit(value_local, "ctx", join_dim=0)
     piece_rows = key_piece.shape[0]
     block_rows = math.gcd(piece_rows, 512)
 

time: 62.2 us -> 55 us (0.88)
  blocking collectives: 12.1 us -> 6.47 us
  matrix products: 4.5 us -> 2.49 us
  local copies, waits for them, and re-layouts: 9.12 us -> 7.27 us
  starting transfers between devices: 21.2 us -> 22.6 us
  waiting for transfers between devices: 8.19 us -> 9.23 us
    all_gather x1 -> x0, blocking collectives: 5.84 us -> none  [body(): value_piece = lax.all_gather(value_local, 'ctx', axis=0, tiled=True)]
    ppermute x0 -> x2, starting transfers between devices: none -> 2.19 us  [map_unit(): jax.lax.ppermute(piece_now, a_name, [(ii, (ii - arr_out) % fresh) for ii...]
    ppermute x0 -> x2, waiting for transfers between devices: none -> 1.9 us  [map_unit(): jax.lax.ppermute(piece_now, a_name, [(ii, (ii - arr_out) % fresh) for ii...]
    all_to_all x1, waiting for transfers between devices: 1.61 us -> 0.01 us  [body(): lax.all_to_all(values, 'head', split_axis=1, concat_axis=0, tiled=True)]
    dot_general x1, matrix products: 1.63 us -> 0.49 us  [update(): jnp.einsum('rkgd,nkd->rkgn', query_grouped, key_head_rows, preferred_elem...]
    all_to_all x1, starting transfers between devices: 3.32 us -> 4.23 us  [body(): lax.all_to_all(values, 'head', split_axis=1, concat_axis=0, tiled=True)]
    all_to_all x1, starting transfers between devices: 4.23 us -> 3.33 us  [body(): lax.all_to_all(keys, 'head', split_axis=1, concat_axis=0, tiled=True)]
    dot_general x1, matrix products: 1.56 us -> 0.69 us  [update(): jnp.einsum('rkgn,nkd->rkgd', weights.astype(jnp.bfloat16), value_head_row...]
  transfers between devices with their start and end apart: 7 -> 9, of which waited for: 2 -> 3; matrix products, arithmetic and copies ran while one was open for 12% -> 13% of each run, Pallas kernels for 0% -> 0%
where the time goes in v1:
time: 55 us; the launch traced here: 54.4 us
  starting transfers between devices  22.6 us (41%)
  waiting for transfers between devices  9.23 us (17%)
  local copies, waits for them, and re-layouts  7.27 us (13%)
  blocking collectives  6.47 us (12%)
  other arithmetic  4.84 us (9%)
  matrix products  2.49 us (5%)
  between operations  1.41 us (3%)
    all_to_all x1, waiting for transfers between devices, body(): lax.all_to_all(gated, 'head', split_axis=0, concat_axis=1, tiled=True)  6.54 us
    all_gather x1, blocking collectives, body(): key_piece = lax.all_gather(key_local, 'ctx', axis=0, tiled=True)  6.47 us
    ppermute x3, starting transfers between devices, from_behind(): return lax.ppermute(block, axis, route)  5.89 us
    all_to_all x1, starting transfers between devices, body(): lax.all_to_all(values, 'head', split_axis=1, concat_axis=0, tiled=True)  4.23 us
    all_to_all x1, starting transfers between devices, body(): lax.all_to_all(gated, 'head', split_axis=0, concat_axis=1, tiled=True)  3.48 us
    all_to_all x1, starting transfers between devices, body(): lax.all_to_all(queries, 'head', split_axis=1, concat_axis=0, tiled=True)  3.47 us
    all_to_all x1, starting transfers between devices, body(): lax.all_to_all(keys, 'head', split_axis=1, concat_axis=0, tiled=True)  3.33 us
    ppermute x2, starting transfers between devices, map_unit(): jax.lax.ppermute(piece_now, a_name, [(ii, (ii - arr_out) % fresh) for ii...  2.19 us
  transfers between devices with their start and end apart: 9, of which 3 were waited for; matrix products, arithmetic and copies ran while one was open for 13% of the time, Pallas kernels for 0%

profile of v1, /device:TPU:0, one launch (start us, length us, event | category | flops | bytes accessed | tf_op | source)
XLA Modules:
  0.0 54.4 jit_solution(9873054976987318285)
XLA Ops:
  0.6 1.5 %copy.90 = bf16[4,2,8,512]{3,2,0,1:T(8,128)(2,1)} copy(bf16[4,2,8,512]{3,2,1,0:T(8,128)(2,1)} %bitcast.48) | data formatting | bytes 131072 | tf_op jit(solution)/shard_map/all_to_all | solution.py:54
  2.2 4.2 %all-to-all-start.2 = ((bf16[32,2,512]{2,0,1:T(8,128)(2,1)}), bf16[32,2,512]{2,0,1:T(8,128)(2,1)S(1)}, u32[]{:S(2)}, u32[]{:S(2)}) async-start(bf16[32,2,512]{2,0,1:T(8,128)(2,1)} %bitcast.35), calls=%async_computation.2 | async-start | bytes 131072 | tf_op jit(solution)/shard_map/all_to_all | solution.py:54
  6.4 0.8 %select_reduce_fusion = s32[64,4]{0,1:T(4,128)S(1)} fusion(s32[4,4]{1,0:T(4,128)} %param.14, pred[64,4]{0,1:T(4,128)(4,1)S(1)} %iota_compare_fusion.3), kind=kLoop, calls=%fused_computation.40 | loop fusion | flops 1792 | bytes 1344 | tf_op jit(solution)/shard_map/reduce_sum | solution.py:64
  7.3 0.7 %select_reduce_fusion.1 = s32[256]{0:T(256)S(1)} fusion(s32[4]{0:T(128)} %param.15, s32[256]{0:T(256)S(1)} %and_select_fusion.2), kind=kLoop, calls=%fused_computation.41 | loop fusion | flops 2816 | bytes 2064 | tf_op jit(solution)/shard_map/while/body/eval_jaxpr/reduce_sum | solution.py:71
  8.2 0.8 %select_reduce_fusion.2 = (s32[64]{0:T(128)S(1)}, s32[64]{0:T(128)S(1)}) fusion(s32[4]{0:T(128)} %param.13, s32[64]{0:T(128)S(1)} %and_select_fusion.3, s32[4]{0:T(128)} %param.15), kind=kLoop, calls=%fused_computation.44 | loop fusion | flops 1152 | bytes 800 | tf_op jit(solution)/shard_map/reduce_sum | solution.py:65
  9.0 0.6 %and_reduce_fusion.2 = pred[]{:T(512)} fusion(pred[4]{0:T(512)(128)(4,1)S(1)} %get-tuple-element.372, pred[4]{0:T(512)(128)(4,1)S(1)} %get-tuple-element.382), kind=kLoop, calls=%fused_computation.50 | loop fusion | flops 7 | bytes 9 | tf_op jit(solution)/shard_map/while/body/eval_jaxpr/reduce_or | solution.py:80
  9.6 1.8 %copy.89 = bf16[4,2,8,3072]{3,2,0,1:T(8,128)(2,1)} copy(bf16[4,2,8,3072]{3,2,1,0:T(8,128)(2,1)} %bitcast.44) | data formatting | bytes 786432 | tf_op jit(solution)/shard_map/all_to_all | solution.py:52
  11.4 1.5 %copy.91 = bf16[4,2,8,512]{3,2,0,1:T(8,128)(2,1)} copy(bf16[4,2,8,512]{3,2,1,0:T(8,128)(2,1)} %bitcast.49) | data formatting | bytes 131072 | tf_op jit(solution)/shard_map/all_to_all | solution.py:53
  13.5 3.3 %all-to-all-start = ((bf16[32,2,512]{2,0,1:T(8,128)(2,1)}), bf16[32,2,512]{2,0,1:T(8,128)(2,1)S(1)}, u32[]{:S(2)}, u32[]{:S(2)}) async-start(bf16[32,2,512]{2,0,1:T(8,128)(2,1)} %bitcast.36), calls=%async_computation | async-start | bytes 131072 | tf_op jit(solution)/shard_map/all_to_all | solution.py:53
  16.9 1.6 %collective-permute-start = (bf16[64,512]{1,0:T(8,128)(2,1)S(1)}, bf16[64,512]{1,0:T(8,128)(2,1)S(1)}, u32[]{:S(2)}, u32[]{:S(2)}) collective-permute-start(bf16[64,512]{1,0:T(8,128)(2,1)S(1)} %bitcast.39), channel_id=1, source_target_pairs={{0,24},{8,0},{16,8},{24,16},{1,25},{9,1},{17,9},{25,17},{2,26},{10... | collective-permute-start | bytes 196616 | tf_op jit(solution)/shard_map/ppermute | solution.py:23
  18.4 1.9 %collective-permute-done = bf16[64,512]{1,0:T(8,128)(2,1)S(1)} collective-permute-done((bf16[64,512]{1,0:T(8,128)(2,1)S(1)}, bf16[64,512]{1,0:T(8,128)(2,1)S(1)}, u32[]{:S(2)}, u32[]{:S(2)}) %collective-permute-start) | collective-permute-done | bytes 65568 | tf_op jit(solution)/shard_map/ppermute | solution.py:23
  20.3 0.6 %collective-permute-start.1 = (bf16[128,512]{1,0:T(8,128)(2,1)S(1)}, bf16[128,512]{1,0:T(8,128)(2,1)S(1)}, u32[]{:S(2)}, u32[]{:S(2)}) collective-permute-start(bf16[128,512]{1,0:T(8,128)(2,1)S(1)} %pad_maximum_fusion), channel_id=1, source_target_pairs={{0,16},{8,24},{16,0},{24,8},{1,17},{9,25},{17,1},{25,9},{2,18},{10... | collective-permute-start | bytes 393224 | tf_op jit(solution)/shard_map/ppermute | solution.py:23
  21.0 3.5 %all-to-all-start.1 = ((bf16[32,2,3072]{2,0,1:T(8,128)(2,1)}), bf16[32,2,3072]{2,0,1:T(8,128)(2,1)S(1)}, u32[]{:S(2)}, u32[]{:S(2)}) async-start(bf16[32,2,3072]{2,0,1:T(8,128)(2,1)} %bitcast.34), calls=%async_computation.1 | async-start | bytes 786432 | tf_op jit(solution)/shard_map/all_to_all | solution.py:52
  24.5 6.5 %all_gather.3 = bf16[256,512]{1,0:T(8,128)(2,1)S(1)} all-gather(bf16[64,512]{1,0:T(8,128)(2,1)S(1)} %bitcast.46), channel_id=1, replica_groups=mesh['ctx'=4,'head'=2,'dp'=4] {'ctx'}, dimensions={0}, use_global_device_ids=true | all-gather | bytes 327680 | tf_op jit(solution)/shard_map/all_gather | solution.py:129
  31.0 0.8 %all-to-all-done.1 = bf16[32,2,3072]{2,0,1:T(8,128)(2,1)S(1)} async-done(((bf16[32,2,3072]{2,0,1:T(8,128)(2,1)}), bf16[32,2,3072]{2,0,1:T(8,128)(2,1)S(1)}, u32[]{:S(2)}, u32[]{:S(2)}) %all-to-all-start.1) | async-done | bytes 393248 | tf_op jit(solution)/shard_map/all_to_all | solution.py:52
  31.8 2.9 %conditional.1 = ((f32[64,4,6]{0,2,1:T(8,128)S(1)}, f32[64,4,6,128]{3,0,2,1:T(8,128)S(1)})) conditional(s32[]{:T(128)} %convert_element_type.15, (f32[64,4,6]{0,2,1:T(8,128)S(1)}, f32[64,4,6,128]{3,0,2,1:T(8,128)S(1)}) %tuple.43, (pred[64,4]{0,1:T(4,128)(4,1)S(1)}, pred[256,4]{0,1:T(4,128)(4,1)S(1)}, s32[256]{0:T(256)S(1)}, s32[256]{0:T(256)S(1)}, ...), branch_computations={%region_6.7_spmd, %region_7.11_spmd.clone} | conditional | flops 205395968 | bytes 10270647 | solution.py:114
  31.8 0.2 copy.65
  32.3 0.5 reshape.159
  32.9 0.5 fusion.20
  33.4 0.6 %fusion.2 = f32[64,4,6]{0,2,1:T(8,128)S(1)} fusion(f32[64,4,6,256]{3,0,2,1:T(8,128)S(1)} %get-tuple-element.377, f32[64,4,6]{0,2,1:T(8,128)S(1)} %broadcast_maximum_fusion, pred[64,256]{1,0:T(8,128)(4,1)S(1)} %broadcast_and_fusion), kind=kLoop, calls=%fused_computation.5 | loop fusion | flops 1178112 | bytes 1601536 | tf_op jit(solution)/shard_map/while/body/eval_jaxpr/cond/branch_1_fun/reduce_sum | solution.py:102
  34.0 0.7 %fusion = f32[64,4,6,128]{3,0,2,1:T(8,128)S(1)} fusion(bf16[256,4,128,1]{0,2,3,1:T(8,128)(2,1)S(1)} %bitcast.43, f32[64,4,6,256]{3,0,2,1:T(8,128)S(1)} %get-tuple-element.377, f32[64,4,6,128]{3,0,2,1:T(8,128)S(1)} %get-tuple-element.272, f32[64,4,6]{0,2,1:T(8,128)S(1)} %broadcast_maximum_fusion, pred[64,256]{1,0:T(8,128)(4,1)S(1)} %broadcast_and_fusion, ...), kind=kOutput, calls=%fused_computation.3 | convolution fusion | flops 102236160 | bytes 3436544 | tf_op jit(solution)/shard_map/while/body/eval_jaxpr/cond/branch_1_fun/rkgn,nkd->rkgd/dot_general | solution.py:103
  34.7 0.3 broadcast_divide_fusion
  34.9 0.5 copy.66
  35.4 0.2 reshape.157
  35.6 1.3 %broadcast_select_fusion = (bf16[64,3072]{1,0:T(8,128)(2,1)S(1)}, bf16[64,3072]{1,0:T(8,128)(2,1)}) fusion(pred[]{:T(512)S(6)} %lt.71, f32[64,3072]{1,0:T(8,128)S(1)} %reshape.157, f32[64,3072]{1,0:T(8,128)S(1)} %copy-done, s32[64]{0:T(128)S(1)} %get-tuple-element.370, pred[64]{0:T(512)(128)(4,1)S(1)} %fusion.18), kind=kOutput, calls=%fused_computation.25 | convolution fusion | flops 151785472 | bytes 2359617 | tf_op jit(solution)/shard_map/dot_general | solution.py:144
  37.0 2.6 %collective-permute-start.2 = (bf16[16,3072]{1,0:T(8,128)(2,1)S(1)}, bf16[16,3072]{1,0:T(8,128)(2,1)S(1)}, u32[]{:S(2)}, u32[]{:S(2)}) collective-permute-start(bf16[16,3072]{1,0:T(8,128)(2,1)S(1)} %get-tuple-element.380), channel_id=1, source_target_pairs={{0,24},{1,25},{2,26},{3,27},{4,28},{5,29},{6,30},{7,31}} | collective-permute-start | bytes 294920 | tf_op jit(solution)/shard_map/ppermute | solution.py:37
  39.5 1.8 %collective-permute-start.3 = (bf16[16,3072]{1,0:T(8,128)(2,1)S(1)}, bf16[16,3072]{1,0:T(8,128)(2,1)S(1)}, u32[]{:S(2)}, u32[]{:S(2)}) collective-permute-start(bf16[16,3072]{1,0:T(8,128)(2,1)S(1)} %get-tuple-element.379), channel_id=1, source_target_pairs={{0,16},{8,24},{1,17},{9,25},{2,18},{10,26},{3,19},{11,27},{4,20},{... | collective-permute-start | bytes 294920 | tf_op jit(solution)/shard_map/ppermute | solution.py:37
  41.4 1.5 %collective-permute-start.4 = (bf16[16,3072]{1,0:T(8,128)(2,1)S(1)}, bf16[16,3072]{1,0:T(8,128)(2,1)S(1)}, u32[]{:S(2)}, u32[]{:S(2)}) collective-permute-start(bf16[16,3072]{1,0:T(8,128)(2,1)S(1)} %get-tuple-element.378), channel_id=1, source_target_pairs={{0,8},{8,16},{16,24},{1,9},{9,17},{17,25},{2,10},{10,18},{18,26},{... | collective-permute-start | bytes 294920 | tf_op jit(solution)/shard_map/ppermute | solution.py:37
  42.9 3.5 %all-to-all-start.3 = ((bf16[2,32,3072]{2,1,0:T(8,128)(2,1)}), bf16[2,32,3072]{2,1,0:T(8,128)(2,1)S(1)}, u32[]{:S(2)}, u32[]{:S(2)}) async-start(bf16[2,32,3072]{2,1,0:T(8,128)(2,1)} %bitcast.6), calls=%async_computation.3 | async-start | bytes 786432 | tf_op jit(solution)/shard_map/all_to_all | solution.py:151
  46.4 0.7 %fusion.14 = bf16[16,3072]{1,0:T(8,128)(2,1)} fusion(bf16[16,3072]{1,0:T(8,128)(2,1)S(1)} %collective-permute-done.2, bf16[16,3072]{1,0:T(8,128)(2,1)S(1)} %collective-permute-done.3, bf16[16,3072]{1,0:T(8,128)(2,1)S(1)} %collective-permute-done.4, bf16[64,3072]{1,0:T(8,128)(2,1)S(1)} %get-tuple-element.383, pred[]{:T(512)S(6)} %eq.100, pred[]{:T(512)S(6)} %eq.99, ...), kind=kLoop, calls=%fused_computation.29 | loop fusion | flops 147456 | bytes 491523 | tf_op jit(solution)/shard_map/jit(_where)/select_n | solution.py:171
  47.1 6.5 %all-to-all-done.3 = bf16[2,32,3072]{2,1,0:T(8,128)(2,1)S(1)} async-done(((bf16[2,32,3072]{2,1,0:T(8,128)(2,1)}), bf16[2,32,3072]{2,1,0:T(8,128)(2,1)S(1)}, u32[]{:S(2)}, u32[]{:S(2)}) %all-to-all-start.3) | async-done | bytes 393248 | tf_op jit(solution)/shard_map/all_to_all | solution.py:151
  53.6 0.8 %copy.77 = bf16[2,4,8,3072]{3,2,0,1:T(8,128)(2,1)} copy(bf16[2,4,8,3072]{3,2,1,0:T(8,128)(2,1)S(1)} %bitcast.38) | data formatting | bytes 786432 | tf_op jit(solution)/shard_map/all_to_all | solution.py:151
  (35 shorter events, 0.8 us)
Async XLA Ops:
  0.6 35.0 %copy-start = (f32[64,3072]{1,0:T(8,128)S(1)}, f32[64,3072]{1,0:T(8,128)}, u32[]{:S(2)}) copy-start(f32[64,3072]{1,0:T(8,128)} %param.12) | copy-start | bytes 2359300
  2.2 11.3 %all-to-all-start.2 = ((bf16[32,2,512]{2,0,1:T(8,128)(2,1)}), bf16[32,2,512]{2,0,1:T(8,128)(2,1)S(1)}, u32[]{:S(2)}, u32[]{:S(2)}) async-start(bf16[32,2,512]{2,0,1:T(8,128)(2,1)} %bitcast.35), calls=%async_computation.2 | async-start | bytes 131072 | tf_op jit(solution)/shard_map/all_to_all | solution.py:54
  13.5 7.5 %all-to-all-start = ((bf16[32,2,512]{2,0,1:T(8,128)(2,1)}), bf16[32,2,512]{2,0,1:T(8,128)(2,1)S(1)}, u32[]{:S(2)}, u32[]{:S(2)}) async-start(bf16[32,2,512]{2,0,1:T(8,128)(2,1)} %bitcast.36), calls=%async_computation | async-start | bytes 131072 | tf_op jit(solution)/shard_map/all_to_all | solution.py:53
  16.9 3.5 %collective-permute-start = (bf16[64,512]{1,0:T(8,128)(2,1)S(1)}, bf16[64,512]{1,0:T(8,128)(2,1)S(1)}, u32[]{:S(2)}, u32[]{:S(2)}) collective-permute-start(bf16[64,512]{1,0:T(8,128)(2,1)S(1)} %bitcast.39), channel_id=1, source_target_pairs={{0,24},{8,0},{16,8},{24,16},{1,25},{9,1},{17,9},{25,17},{2,26},{10... | collective-permute-start | bytes 196616 | tf_op jit(solution)/shard_map/ppermute | solution.py:23
  20.3 10.6 %collective-permute-start.1 = (bf16[128,512]{1,0:T(8,128)(2,1)S(1)}, bf16[128,512]{1,0:T(8,128)(2,1)S(1)}, u32[]{:S(2)}, u32[]{:S(2)}) collective-permute-start(bf16[128,512]{1,0:T(8,128)(2,1)S(1)} %pad_maximum_fusion), channel_id=1, source_target_pairs={{0,16},{8,24},{16,0},{24,8},{1,17},{9,25},{17,1},{25,9},{2,18},{10... | collective-permute-start | bytes 393224 | tf_op jit(solution)/shard_map/ppermute | solution.py:23
  21.0 10.8 %all-to-all-start.1 = ((bf16[32,2,3072]{2,0,1:T(8,128)(2,1)}), bf16[32,2,3072]{2,0,1:T(8,128)(2,1)S(1)}, u32[]{:S(2)}, u32[]{:S(2)}) async-start(bf16[32,2,3072]{2,0,1:T(8,128)(2,1)} %bitcast.34), calls=%async_computation.1 | async-start | bytes 786432 | tf_op jit(solution)/shard_map/all_to_all | solution.py:52
  37.0 9.4 %collective-permute-start.2 = (bf16[16,3072]{1,0:T(8,128)(2,1)S(1)}, bf16[16,3072]{1,0:T(8,128)(2,1)S(1)}, u32[]{:S(2)}, u32[]{:S(2)}) collective-permute-start(bf16[16,3072]{1,0:T(8,128)(2,1)S(1)} %get-tuple-element.380), channel_id=1, source_target_pairs={{0,24},{1,25},{2,26},{3,27},{4,28},{5,29},{6,30},{7,31}} | collective-permute-start | bytes 294920 | tf_op jit(solution)/shard_map/ppermute | solution.py:37
  39.5 6.8 %collective-permute-start.3 = (bf16[16,3072]{1,0:T(8,128)(2,1)S(1)}, bf16[16,3072]{1,0:T(8,128)(2,1)S(1)}, u32[]{:S(2)}, u32[]{:S(2)}) collective-permute-start(bf16[16,3072]{1,0:T(8,128)(2,1)S(1)} %get-tuple-element.379), channel_id=1, source_target_pairs={{0,16},{8,24},{1,17},{9,25},{2,18},{10,26},{3,19},{11,27},{4,20},{... | collective-permute-start | bytes 294920 | tf_op jit(solution)/shard_map/ppermute | solution.py:37
  41.4 5.0 %collective-permute-start.4 = (bf16[16,3072]{1,0:T(8,128)(2,1)S(1)}, bf16[16,3072]{1,0:T(8,128)(2,1)S(1)}, u32[]{:S(2)}, u32[]{:S(2)}) collective-permute-start(bf16[16,3072]{1,0:T(8,128)(2,1)S(1)} %get-tuple-element.378), channel_id=1, source_target_pairs={{0,8},{8,16},{16,24},{1,9},{9,17},{17,25},{2,10},{10,18},{18,26},{... | collective-permute-start | bytes 294920 | tf_op jit(solution)/shard_map/ppermute | solution.py:37
  42.9 10.7 %all-to-all-start.3 = ((bf16[2,32,3072]{2,1,0:T(8,128)(2,1)}), bf16[2,32,3072]{2,1,0:T(8,128)(2,1)S(1)}, u32[]{:S(2)}, u32[]{:S(2)}) async-start(bf16[2,32,3072]{2,1,0:T(8,128)(2,1)} %bitcast.6), calls=%async_computation.3 | async-start | bytes 786432 | tf_op jit(solution)/shard_map/all_to_all | solution.py:151
